TPU v7x, 32 devices: a whole 2x2x4 slice. The times are simulated.
32 devices in a mesh: dp: 8 (over z, core), mp: 4 (over y, x).
Axes of the slice: x: 2, y: 2, z: 4, core: 2. Of those that a mesh axis runs over, the one named last changes fastest.
Arguments:
- tokens: bfloat16 [12288, 2048], P(('dp', 'mp')), may hold values from -6 to 6
- segment_ids: int32 [16, 768], P('dp'), may hold values from 0 to 5, never falling along the last dimension, each value on 1 to 256 neighbouring positions
- query_weight: bfloat16 [2048, 2048], P(None, 'mp'), may hold values from -0.125 to 0.125
- key_weight: bfloat16 [2048, 2048], P(None, 'mp'), may hold values from -0.125 to 0.125
- value_weight: bfloat16 [2048, 2048], P(None, 'mp'), may hold values from -0.125 to 0.125
- out_weight: bfloat16 [2048, 2048], P('mp'), may hold values from -0.75 to 0.75
- up_weight: bfloat16 [2048, 8192], P(None, 'mp'), may hold values from -0.125 to 0.125
- down_weight: bfloat16 [8192, 2048], P('mp'), may hold values from -0.0625 to 0.0625
- attn_gain: float32 [2048], replicated, may hold values from 0.5 to 1.5
- mlp_gain: float32 [2048], replicated, may hold values from 0.5 to 1.5
- out_cotangent: bfloat16 [12288, 2048], P(('dp', 'mp')), may hold values from -18 to 18
Outputs:
- layer_output: bfloat16 [12288, 2048], P(('dp', 'mp'))
- tokens_grad: float32 [12288, 2048], P(('dp', 'mp'))
- query_weight_grad: float32 [2048, 2048], P('dp', 'mp')
- key_weight_grad: float32 [2048, 2048], P('dp', 'mp')
- value_weight_grad: float32 [2048, 2048], P('dp', 'mp')
- out_weight_grad: float32 [2048, 2048], P('mp', 'dp')
- up_weight_grad: float32 [2048, 8192], P('dp', 'mp')
- down_weight_grad: float32 [8192, 2048], P('mp', 'dp')
- attn_gain_grad: float32 [2048], replicated
- mlp_gain_grad: float32 [2048], replicated
Inputs may be any that keep to these rules, and one draw needn't show every extreme that they name: `segment_ids`: within each packed sequence the clip numbers never fall; each clip covers 1 to 256 tokens, and some clip covers exactly 256.
All inputs are finite; a program needn't handle non-finite values.
Results may differ from a plain program's by a relative error of at most 0.02.
Values may be sent and summed in bfloat16 or wider, within the bound.
A program may use at most 192 MiB of HBM per device.

v0:
```python
import math
import jax
import jax.numpy as jnp
from jax import lax
from jax.sharding import PartitionSpec as P

HEAD_DIM = 128
epsilon = 1e-05
masked_score = -1e30


def norm_rows(values, gain):
    centre = jnp.mean(values, axis=-1, keepdims=True)
    centred = values - centre
    spread = jnp.mean(centred * centred, axis=-1, keepdims=True)
    return centred * lax.rsqrt(spread + epsilon) * gain


def gelu_tanh(values):
    return jax.nn.gelu(values, approximate=True)


def block_allowed(segment):
    position = jnp.arange(segment.shape[0])
    return (position[None, :] <= position[:, None]) & (segment[:, None] == segment[None, :])


def rows_times(left_rows, right_matrix):
    return jnp.dot(left_rows, right_matrix, preferred_element_type=jnp.float32)


def rows_times_back(left_rows, right_matrix):
    return lax.dot_general(
        left_rows, right_matrix, (((1,), (1,)), ((), ())), preferred_element_type=jnp.float32
    )


def attn_input_back(
    queries_grad, keys_grad, values_grad, query_weight, key_weight, value_weight, score_scale
):
    total_grad = rows_times_back(queries_grad, query_weight) * score_scale
    total_grad = total_grad + rows_times_back(keys_grad, key_weight)
    return total_grad + rows_times_back(values_grad, value_weight)


def attend_forward(packed):
    queries, keys_in, values_in, segment = packed
    scores = jnp.einsum("qhd,khd->hqk", queries, keys_in, preferred_element_type=jnp.float32)
    scores = jnp.where(block_allowed(segment)[None], scores, masked_score)
    row_max = jnp.max(scores, axis=-1, keepdims=True)
    expanded = jnp.exp(scores - row_max)
    row_total = jnp.sum(expanded, axis=-1, keepdims=True)
    probs_low = (expanded / row_total).astype(jnp.bfloat16)
    context = jnp.einsum("hqk,khd->qhd", probs_low, values_in, preferred_element_type=jnp.float32)
    return (context.astype(jnp.bfloat16), (row_max + jnp.log(row_total))[:, :, 0])


def attend_backward(packed):
    queries, keys_in, values_in, segment, context_grad, log_total = packed
    scores = jnp.einsum("qhd,khd->hqk", queries, keys_in, preferred_element_type=jnp.float32)
    scores = jnp.where(block_allowed(segment)[None], scores, masked_score)
    attn_probs = jnp.exp(scores - log_total[:, :, None])
    probs_grad = jnp.einsum(
        "qhd,khd->hqk", context_grad, values_in, preferred_element_type=jnp.float32
    )
    values_grad = jnp.einsum(
        "hqk,qhd->khd",
        attn_probs.astype(jnp.bfloat16),
        context_grad,
        preferred_element_type=jnp.float32,
    )
    inner_sum = jnp.sum(attn_probs * probs_grad, axis=-1, keepdims=True)
    scores_grad = (attn_probs * (probs_grad - inner_sum)).astype(jnp.bfloat16)
    queries_grad = jnp.einsum(
        "hqk,khd->qhd", scores_grad, keys_in, preferred_element_type=jnp.float32
    )
    keys_grad = jnp.einsum("hqk,qhd->khd", scores_grad, queries, preferred_element_type=jnp.float32)
    return (
        queries_grad.astype(jnp.bfloat16),
        keys_grad.astype(jnp.bfloat16),
        values_grad.astype(jnp.bfloat16),
    )


def local(
    tokens,
    segment_ids,
    query_weight,
    key_weight,
    value_weight,
    out_weight,
    up_weight,
    down_weight,
    attn_gain,
    mlp_gain,
    out_cotangent,
):
    seq_count, seq_length = segment_ids.shape
    group_rows = seq_count * seq_length
    head_count = query_weight.shape[1] // HEAD_DIM
    score_scale = 1.0 / math.sqrt(HEAD_DIM)
    shaped = (seq_count, seq_length, head_count, HEAD_DIM)
    flat_shape = (group_rows, head_count * HEAD_DIM)
    residual_in = tokens.astype(jnp.float32)
    normed_attn, attn_norm_back = jax.vjp(norm_rows, residual_in, attn_gain)
    gathered_attn = lax.all_gather(normed_attn.astype(jnp.bfloat16), "mp", axis=0, tiled=True)
    queries = (
        jnp.dot(gathered_attn, query_weight, preferred_element_type=jnp.float32) * score_scale
    ).astype(jnp.bfloat16)
    keys_all = jnp.dot(gathered_attn, key_weight, preferred_element_type=jnp.float32).astype(
        jnp.bfloat16
    )
    values_all = jnp.dot(gathered_attn, value_weight, preferred_element_type=jnp.float32).astype(
        jnp.bfloat16
    )
    queries_seq = queries.reshape(shaped)
    keys_seq = keys_all.reshape(shaped)
    values_seq = values_all.reshape(shaped)
    context, log_total = lax.map(attend_forward, (queries_seq, keys_seq, values_seq, segment_ids))
    context_flat = context.reshape(flat_shape)
    attn_rows = lax.psum_scatter(
        rows_times(context_flat, out_weight).astype(jnp.bfloat16),
        "mp",
        scatter_dimension=0,
        tiled=True,
    ).astype(jnp.float32)
    residual_mid = residual_in + attn_rows
    normed_mlp, mlp_norm_back = jax.vjp(norm_rows, residual_mid, mlp_gain)
    gathered_mlp = lax.all_gather(normed_mlp.astype(jnp.bfloat16), "mp", axis=0, tiled=True)
    pre_act = jnp.dot(gathered_mlp, up_weight, preferred_element_type=jnp.float32)
    activated, gelu_back = jax.vjp(gelu_tanh, pre_act)
    hidden = activated.astype(jnp.bfloat16)
    mlp_rows = lax.psum_scatter(
        rows_times(hidden, down_weight).astype(jnp.bfloat16), "mp", scatter_dimension=0, tiled=True
    ).astype(jnp.float32)
    layer_output = (residual_mid + mlp_rows).astype(jnp.bfloat16)
    cotangent_all = lax.all_gather(out_cotangent, "mp", axis=0, tiled=True)
    down_weight_grad = jnp.einsum(
        "rf,rd->fd", hidden, cotangent_all, preferred_element_type=jnp.float32
    )
    hidden_grad = lax.dot_general(
        cotangent_all, down_weight, (((1,), (1,)), ((), ())), preferred_element_type=jnp.float32
    )
    pre_grad = gelu_back(hidden_grad)[0].astype(jnp.bfloat16)
    up_weight_grad = jnp.einsum(
        "rd,rf->df", gathered_mlp, pre_grad, preferred_element_type=jnp.float32
    )
    normed_mlp_grad = lax.psum_scatter(
        rows_times_back(pre_grad, up_weight).astype(jnp.bfloat16),
        "mp",
        scatter_dimension=0,
        tiled=True,
    ).astype(jnp.float32)
    middle_back, mlp_gain_grad = mlp_norm_back(normed_mlp_grad)
    middle_grad = out_cotangent.astype(jnp.float32) + middle_back
    middle_all_grad = lax.all_gather(middle_grad.astype(jnp.bfloat16), "mp", axis=0, tiled=True)
    out_weight_grad = jnp.einsum(
        "rc,rd->cd", context_flat, middle_all_grad, preferred_element_type=jnp.float32
    )
    context_grad = lax.dot_general(
        middle_all_grad, out_weight, (((1,), (1,)), ((), ())), preferred_element_type=jnp.float32
    ).astype(jnp.bfloat16)
    queries_grad, keys_grad, values_grad = lax.map(
        attend_backward,
        (queries_seq, keys_seq, values_seq, segment_ids, context_grad.reshape(shaped), log_total),
    )
    queries_grad = queries_grad.reshape(flat_shape)
    keys_grad = keys_grad.reshape(flat_shape)
    values_grad = values_grad.reshape(flat_shape)
    query_weight_grad = (
        jnp.einsum("rd,rc->dc", gathered_attn, queries_grad, preferred_element_type=jnp.float32)
        * score_scale
    )
    key_weight_grad = jnp.einsum(
        "rd,rc->dc", gathered_attn, keys_grad, preferred_element_type=jnp.float32
    )
    value_weight_grad = jnp.einsum(
        "rd,rc->dc", gathered_attn, values_grad, preferred_element_type=jnp.float32
    )
    normed_attn_grad = lax.psum_scatter(
        attn_input_back(
            queries_grad,
            keys_grad,
            values_grad,
            query_weight,
            key_weight,
            value_weight,
            score_scale,
        ).astype(jnp.bfloat16),
        "mp",
        scatter_dimension=0,
        tiled=True,
    ).astype(jnp.float32)
    token_back, attn_gain_grad = attn_norm_back(normed_attn_grad)
    tokens_grad = middle_grad + token_back
    attn_gain_grad, mlp_gain_grad = lax.psum((attn_gain_grad, mlp_gain_grad), ("dp", "mp"))
    (
        query_weight_grad,
        key_weight_grad,
        value_weight_grad,
        out_weight_grad,
        up_weight_grad,
        down_weight_grad,
    ) = (
        lax.psum_scatter(
            query_weight_grad.astype(jnp.bfloat16), "dp", scatter_dimension=0, tiled=True
        ).astype(jnp.float32),
        lax.psum_scatter(
            key_weight_grad.astype(jnp.bfloat16), "dp", scatter_dimension=0, tiled=True
        ).astype(jnp.float32),
        lax.psum_scatter(
            value_weight_grad.astype(jnp.bfloat16), "dp", scatter_dimension=0, tiled=True
        ).astype(jnp.float32),
        lax.psum_scatter(
            out_weight_grad.astype(jnp.bfloat16), "dp", scatter_dimension=1, tiled=True
        ).astype(jnp.float32),
        lax.psum_scatter(
            up_weight_grad.astype(jnp.bfloat16), "dp", scatter_dimension=0, tiled=True
        ).astype(jnp.float32),
        lax.psum_scatter(
            down_weight_grad.astype(jnp.bfloat16), "dp", scatter_dimension=1, tiled=True
        ).astype(jnp.float32),
    )
    return (
        layer_output,
        tokens_grad,
        query_weight_grad,
        key_weight_grad,
        value_weight_grad,
        out_weight_grad,
        up_weight_grad,
        down_weight_grad,
        attn_gain_grad,
        mlp_gain_grad,
    )


def solution(mesh):
    return jax.shard_map(
        local,
        mesh=mesh,
        in_specs=(
            P(("dp", "mp"), None),
            P("dp", None),
            P(None, "mp"),
            P(None, "mp"),
            P(None, "mp"),
            P("mp", None),
            P(None, "mp"),
            P("mp", None),
            P(),
            P(),
            P(("dp", "mp"), None),
        ),
        out_specs=(
            P(("dp", "mp"), None),
            P(("dp", "mp"), None),
            P("dp", "mp"),
            P("dp", "mp"),
            P("dp", "mp"),
            P("mp", "dp"),
            P("dp", "mp"),
            P("mp", "dp"),
            P(),
            P(),
        ),
        check_vma=False,
    )
```

profile of v0, /device:TPU:0, one launch (start us, length us, event | category | flops | bytes accessed | tf_op | source)
XLA Modules:
  0.0 1105.6 jit_solution(7210589673843302547)
XLA Ops:
  14.0 73.0 %all-gather.5.cloned.1.call-done = bf16[1536,2048]{1,0:T(8,128)(2,1)} async-done(((bf16[384,2048]{1,0:T(8,128)(2,1)}), bf16[1536,2048]{1,0:T(8,128)(2,1)}) %all-gather.5.cloned.1.call-update) | async-done | bytes 6291472 | tf_op jit(solution)/shard_map/all_gather | solution.py:106
  87.0 8.0 convolution_convert_fusion.11
  94.9 3.7 reshape.216
  101.6 7.3 fusion.63
  115.3 7.3 convolution_convert_fusion.12
  127.6 28.2 %while.26 = (s32[]{:T(128)}, bf16[2,768,4,128]{3,2,1,0:T(4,128)(2,1)}, f32[2,4,768]{2,1,0:T(4,128)S(1)}, bf16[2,768,4,128]{3,2,1,0:T(4,128)(2,1)}, s32[2,768]{1,...) while((s32[]{:T(128)}, ...), condition=%wide.region_5.6_spmd, body=%wide.region_2.5_spmd.sunk | while | flops 1231352832 | bytes 43362440 | solution.py:119
  135.4 3.6 fusion.137
  149.5 3.6 fusion.137
  155.8 7.2 convolution_convert_fusion.6
  163.8 69.6 %reduce-scatter.11.cloned.1.call-done = bf16[384,2048]{1,0:T(8,128)(2,1)} async-done(((bf16[1536,2048]{1,0:T(8,128)(2,1)}), bf16[384,2048]{1,0:T(8,128)(2,1)}) %reduce-scatter.11.cloned.1.call-update) | async-done | bytes 1572880 | tf_op jit(solution)/shard_map/reduce_scatter | solution.py:121
  238.9 66.6 %all-gather.9.cloned.1.call-done = bf16[1536,2048]{1,0:T(8,128)(2,1)} async-done(((bf16[384,2048]{1,0:T(8,128)(2,1)}), bf16[1536,2048]{1,0:T(8,128)(2,1)}) %all-gather.9.cloned.1.call-update) | async-done | bytes 6291472 | tf_op jit(solution)/shard_map/all_gather | solution.py:137
  305.5 19.1 %fusion.89 = f32[1536,2048]{1,0:T(8,128)} fusion(bf16[1536,2048]{1,0:T(8,128)(2,1)} %all-gather.9.cloned.1.call-done, bf16[2048,2048]{1,0:T(8,128)(2,1)} %param.22), kind=kOutput, calls=%fused_computation.146 | convolution fusion | flops 12884901888 | bytes 27262976 | tf_op jit(solution)/shard_map/dot_general | solution.py:141
  324.5 53.4 %all-gather.7.cloned.1.call-done = bf16[1536,2048]{1,0:T(8,128)(2,1)} async-done(((bf16[384,2048]{1,0:T(8,128)(2,1)}), bf16[1536,2048]{1,0:T(8,128)(2,1)}) %all-gather.7.cloned.1.call-update) | async-done | bytes 6291472 | tf_op jit(solution)/shard_map/all_gather | solution.py:129
  377.9 29.6 %fusion.48 = (bf16[1536,2048]{1,0:T(8,128)(2,1)}, f32[1536,2048]{1,0:T(8,128)}) fusion(f32[1536,2048]{1,0:T(8,128)} %fusion.89, bf16[1536,2048]{1,0:T(8,128)(2,1)} %all-gather.7.cloned.1.call-done, bf16[2048,2048]{1,0:T(8,128)(2,1)} %param.21), kind=kOutput, calls=%fused_computation.68 | convolution fusion | flops 12947816448 | bytes 46137344 | tf_op jit(solution)/shard_map/dot_general | solution.py:130
  407.5 19.1 %convolution_convert_fusion.4 = bf16[1536,2048]{1,0:T(8,128)(2,1)} fusion(bf16[1536,2048]{1,0:T(8,128)(2,1)} %get-tuple-element.190, bf16[2048,2048]{1,0:T(8,128)(2,1)} %param.21), kind=kOutput, calls=%fused_computation.73 | convolution fusion | flops 12888047616 | bytes 20971520 | tf_op jit(solution)/shard_map/dot_general | solution.py:33
  426.7 20.5 %convolution_convert_fusion.5 = bf16[1536,2048]{1,0:T(8,128)(2,1)} fusion(bf16[2048,2048]{1,0:T(8,128)(2,1)} %param.22, f32[1536,2048]{1,0:T(8,128)} %get-tuple-element.191), kind=kOutput, calls=%fused_computation.74 | convolution fusion | flops 12916359168 | bytes 27262976 | tf_op jit(solution)/shard_map/dot_general | solution.py:29
  447.3 49.7 %reduce-scatter.15.cloned.1.call-done = bf16[384,2048]{1,0:T(8,128)(2,1)} async-done(((bf16[1536,2048]{1,0:T(8,128)(2,1)}), bf16[384,2048]{1,0:T(8,128)(2,1)}) %reduce-scatter.15.cloned.1.call-update) | async-done | bytes 1572880 | tf_op jit(solution)/shard_map/reduce_scatter | solution.py:148
  497.0 4.4 fusion.59
  501.4 68.7 %reduce-scatter.13.cloned.1.call-done = bf16[384,2048]{1,0:T(8,128)(2,1)} async-done(((bf16[1536,2048]{1,0:T(8,128)(2,1)}), bf16[384,2048]{1,0:T(8,128)(2,1)}) %reduce-scatter.13.cloned.1.call-update) | async-done | bytes 1572880 | tf_op jit(solution)/shard_map/reduce_scatter | solution.py:133
  570.1 5.5 fusion.88
  578.9 19.6 %convolution_convert_fusion.3 = bf16[2048,2048]{1,0:T(8,128)(2,1)} fusion(bf16[1536,2048]{1,0:T(8,128)(2,1)} %all-gather.7.cloned.1.call-done, bf16[1536,2048]{1,0:T(8,128)(2,1)} %get-tuple-element.190), kind=kOutput, calls=%fused_computation.72 | convolution fusion | flops 12889096192 | bytes 20971520 | tf_op jit(solution)/shard_map/rd,rf->df/dot_general | solution.py:145
  598.5 22.5 %convolution_convert_fusion.2 = bf16[2048,2048]{1,0:T(8,128)(2,1)} fusion(bf16[1536,2048]{1,0:T(8,128)(2,1)} %all-gather.9.cloned.1.call-done, f32[1536,2048]{1,0:T(8,128)} %get-tuple-element.191), kind=kOutput, calls=%fused_computation.71 | convolution fusion | flops 12917407744 | bytes 27262976 | tf_op jit(solution)/shard_map/rf,rd->fd/dot_general | solution.py:138
  621.1 28.0 %all-gather.11.cloned.1.call-done = bf16[1536,2048]{1,0:T(8,128)(2,1)} async-done(((bf16[384,2048]{1,0:T(8,128)(2,1)}), bf16[1536,2048]{1,0:T(8,128)(2,1)}) %all-gather.11.cloned.1.call-update) | async-done | bytes 6291472 | tf_op jit(solution)/shard_map/all_gather | solution.py:156
  649.1 7.8 convolution_convert_fusion.10
  657.0 3.7 reshape.218
  660.6 8.1 convolution_convert_fusion.7
  673.6 99.9 %while.27 = (s32[]{:T(128)}, bf16[2,768,4,128]{3,2,1,0:T(4,128)(2,1)}, bf16[2,768,4,128]{3,2,1,0:T(4,128)(2,1)}, bf16[2,768,4,128]{3,2,1,0:T(4,128)(2,1)}, bf16[...) while((s32[]{:T(128)}, ...), condition=%wide.region_15.16_spmd, body=%wide.region_13.15_spmd.sunk | while | flops 3051156480 | bytes 169179440 | solution.py:163
  679.6 3.6 copy-done.1
  689.0 8.2 multiply_reduce_fusion.3
  697.2 10.9 multiply_convert_fusion.7
  708.1 4.5 fusion.149
  729.1 3.6 copy-done.1
  738.5 8.1 multiply_reduce_fusion.3
  746.6 11.5 %multiply_convert_fusion.7 = bf16[4,768,768]{1,2,0:T(8,128)(2,1)} fusion(f32[4,768,768]{1,2,0:T(8,128)} %get-tuple-element.304, f32[4,768,768]{1,2,0:T(8,128)} %copy-done.1, f32[4,768]{1,0:T(4,128)S(1)} %get-tuple-element.305, f32[4,768]{1,0:T(4,128)S(1)} %dynamic-slice_bitcast_fusion.2, pred[768,768]{0,1:T(8,128)(4,1)S(1)} %fusion.146), kind=kLoop, calls=%fused_computation.21.clone.1 | loop fusion | flops 11796480 | bytes 24207360 | tf_op jit(solution)/shard_map/while/body/eval_jaxpr/convert_element_type | solution.py:73
  758.1 4.4 fusion.149
  773.5 8.1 multiply_convert_fusion.2
  781.7 8.1 convolution_convert_fusion.8
  789.8 8.1 convolution_convert_fusion.9
  798.3 10.2 fusion.72
  808.5 6.5 fusion.69
  815.0 15.8 %add_convert_fusion = bf16[1536,2048]{1,0:T(8,128)(2,1)} fusion(f32[1536,2048]{1,0:T(8,128)} %fusion.69, f32[1536,2048]{1,0:T(8,128)} %fusion.72, bf16[2048,512]{1,0:T(8,128)(2,1)} %param.17, bf16[192,8,4,128]{3,2,1,0:T(4,128)(2,1)} %bitcast.147), kind=kOutput, calls=%fused_computation.69 | convolution fusion | flops 3233808384 | bytes 35127296 | tf_op jit(solution)/shard_map/dot_general | solution.py:33
  836.4 31.3 %reduce-scatter.25.cloned.1.call-done = bf16[512,256]{1,0:T(8,128)(2,1)} async-done(((bf16[512,2048]{1,0:T(8,128)(2,1)}), bf16[512,256]{1,0:T(8,128)(2,1)}) %reduce-scatter.25.cloned.1.call-update) | async-done | bytes 262160 | tf_op jit(solution)/shard_map/reduce_scatter | solution.py:214
  869.4 34.9 %reduce-scatter.19.cloned.1.call-done = bf16[256,512]{1,0:T(8,128)(2,1)} async-done(((bf16[2048,512]{1,0:T(8,128)(2,1)}), bf16[256,512]{1,0:T(8,128)(2,1)}) %reduce-scatter.19.cloned.1.call-update) | async-done | bytes 262160 | tf_op jit(solution)/shard_map/reduce_scatter | solution.py:205
  906.1 34.9 %reduce-scatter.23.cloned.1.call-done = bf16[256,512]{1,0:T(8,128)(2,1)} async-done(((bf16[2048,512]{1,0:T(8,128)(2,1)}), bf16[256,512]{1,0:T(8,128)(2,1)}) %reduce-scatter.23.cloned.1.call-update) | async-done | bytes 262160 | tf_op jit(solution)/shard_map/reduce_scatter | solution.py:211
  942.9 34.9 %reduce-scatter.21.cloned.1.call-done = bf16[256,512]{1,0:T(8,128)(2,1)} async-done(((bf16[2048,512]{1,0:T(8,128)(2,1)}), bf16[256,512]{1,0:T(8,128)(2,1)}) %reduce-scatter.21.cloned.1.call-update) | async-done | bytes 262160 | tf_op jit(solution)/shard_map/reduce_scatter | solution.py:208
  979.6 70.0 %reduce-scatter.17.cloned.1.call-done = bf16[384,2048]{1,0:T(8,128)(2,1)} async-done(((bf16[1536,2048]{1,0:T(8,128)(2,1)}), bf16[384,2048]{1,0:T(8,128)(2,1)}) %reduce-scatter.17.cloned.1.call-update) | async-done | bytes 1572880 | tf_op jit(solution)/shard_map/reduce_scatter | solution.py:180
  1054.0 39.5 %all-reduce = (f32[2048]{0:T(1024)}, f32[2048]{0:T(1024)}) all-reduce(f32[2048]{0:T(1024)S(1)} %get-tuple-element.143, f32[2048]{0:T(1024)S(1)} %copy-done.27), channel_id=1, replica_groups=mesh['dp'=8,'mp'=4] {'dp','mp'}, use_global_device_ids=true, to_apply=%region_26.27 | all-reduce | flops 4096 | bytes 32768 | tf_op jit(solution)/shard_map/psum | solution.py:196
  1093.5 5.1 add_add_fusion.2
  (184 shorter events, 118.7 us)
Async XLA Ops:
  7.2 148.6 %copy-start = (bf16[512,2048]{1,0:T(8,128)(2,1)S(1)}, bf16[512,2048]{1,0:T(8,128)(2,1)}, u32[]{:S(2)}) copy-start(bf16[512,2048]{1,0:T(8,128)(2,1)} %param.20) | copy-start | bytes 6291460
  7.2 5.0 copy-start.20
  7.2 79.8 %all-gather.5.cloned.1.call-start = ((), (), s32[]{:S(2)}) async-start(), calls=%async_computation.10 | async-start | bytes 7864320 | tf_op jit(solution)/shard_map/all_gather | solution.py:106
  7.2 5.0 copy-start.3
  9.1 2.5 copy-start.22
  13.9 219.5 %reduce-scatter.11.cloned.1.call-start = ((), (), s32[]{:S(2)}) async-start(), calls=%async_computation.11 | async-start | bytes 7864320 | tf_op jit(solution)/shard_map/reduce_scatter | solution.py:121
  98.6 2.9 copy-start.14
  112.4 2.9 copy-start.32
  122.6 5.1 copy-start.18
  155.8 7.2 copy-start.16
  163.1 142.4 %all-gather.9.cloned.1.call-start = ((), (), s32[]{:S(2)}) async-start(), calls=%async_computation.14 | async-start | bytes 7864320 | tf_op jit(solution)/shard_map/all_gather | solution.py:137
  163.1 73.9 %copy-start.24 = (f32[2048]{0:T(1024)S(1)}, f32[2048]{0:T(1024)}, u32[]{:S(2)}) copy-start(f32[2048]{0:T(1024)} %param.24) | copy-start | bytes 24580
  163.8 214.1 %all-gather.7.cloned.1.call-start = ((), (), s32[]{:S(2)}) async-start(), calls=%async_computation.12 | async-start | bytes 7864320 | tf_op jit(solution)/shard_map/all_gather | solution.py:129
  233.4 2.5 copy-start.4
  233.4 2.8 copy-start.9
  238.8 258.2 %reduce-scatter.15.cloned.1.call-start = ((), (), s32[]{:S(2)}) async-start(), calls=%async_computation.15 | async-start | bytes 7864320 | tf_op jit(solution)/shard_map/reduce_scatter | solution.py:148
  426.7 143.4 %reduce-scatter.13.cloned.1.call-start = ((), (), s32[]{:S(2)}) async-start(), calls=%async_computation.13 | async-start | bytes 7864320 | tf_op jit(solution)/shard_map/reduce_scatter | solution.py:133
  447.2 201.9 %all-gather.11.cloned.1.call-start = ((), (), s32[]{:S(2)}) async-start(), calls=%async_computation.16 | async-start | bytes 7864320 | tf_op jit(solution)/shard_map/all_gather | solution.py:156
  570.1 7.2 copy-start.13
  578.8 252.0 %reduce-scatter.27.cloned.1.call-start = ((), (), s32[]{:S(2)}) async-start(), calls=%async_computation.22 | async-start | bytes 9437184 | tf_op jit(solution)/shard_map/reduce_scatter | solution.py:217
  598.5 235.2 %reduce-scatter.29.cloned.1.call-start = ((), (), s32[]{:S(2)}) async-start(), calls=%async_computation.23 | async-start | bytes 9437184 | tf_op jit(solution)/shard_map/reduce_scatter | solution.py:220
  621.0 246.6 %reduce-scatter.25.cloned.1.call-start = ((), (), s32[]{:S(2)}) async-start(), calls=%async_computation.21 | async-start | bytes 2359296 | tf_op jit(solution)/shard_map/reduce_scatter | solution.py:214
  668.8 4.8 copy-start.17
  668.8 4.8 copy-start.19
  668.8 235.5 %reduce-scatter.19.cloned.1.call-start = ((), (), s32[]{:S(2)}) async-start(), calls=%async_computation.18 | async-start | bytes 2359296 | tf_op jit(solution)/shard_map/reduce_scatter | solution.py:205
  673.8 4.4 copy-start.6
  673.8 4.4 copy-start.8
  679.6 3.6 copy-start.1
  708.1 4.5 copy-start.2
  708.1 4.6 copy-start.7
  723.3 4.5 copy-start.6
  723.3 4.5 copy-start.8
  729.1 3.6 copy-start.1
  758.1 4.4 copy-start.2
  758.1 4.6 copy-start.7
  781.6 159.5 %reduce-scatter.23.cloned.1.call-start = ((), (), s32[]{:S(2)}) async-start(), calls=%async_computation.20 | async-start | bytes 2359296 | tf_op jit(solution)/shard_map/reduce_scatter | solution.py:211
  789.8 188.0 %reduce-scatter.21.cloned.1.call-start = ((), (), s32[]{:S(2)}) async-start(), calls=%async_computation.19 | async-start | bytes 2359296 | tf_op jit(solution)/shard_map/reduce_scatter | solution.py:208
  798.0 251.6 %reduce-scatter.17.cloned.1.call-start = ((), (), s32[]{:S(2)}) async-start(), calls=%async_computation.17 | async-start | bytes 7864320 | tf_op jit(solution)/shard_map/reduce_scatter | solution.py:180
  798.3 10.2 copy-start.15
  798.3 10.2 copy-start.33
  833.6 215.9 %copy-start.21 = (f32[2048]{0:T(1024)S(1)}, f32[2048]{0:T(1024)}, u32[]{:S(2)}) copy-start(f32[2048]{0:T(1024)} %param.23) | copy-start | bytes 24580
  833.6 215.9 %copy-start.23 = (f32[384]{0:T(512)S(1)}, f32[384]{0:T(512)}, u32[]{:S(2)}) copy-start(f32[384]{0:T(512)} %copy-done.22) | copy-start | bytes 4612
  836.4 216.0 %copy-start.31 = (f32[384]{0:T(512)S(1)}, f32[384]{0:T(512)}, u32[]{:S(2)}) copy-start(f32[384]{0:T(512)} %copy-done.30) | copy-start | bytes 4612
  836.4 216.0 %copy-start.26 = (f32[384]{0:T(512)S(1)}, f32[384]{0:T(512)}, u32[]{:S(2)}) copy-start(f32[384]{0:T(512)} %copy-done.25) | copy-start | bytes 4612
  979.6 74.4 %copy-start.27 = (f32[2048]{0:T(1024)S(1)}, f32[2048]{0:T(1024)}, u32[]{:S(2)}) copy-start(f32[2048]{0:T(1024)} %get-tuple-element.141) | copy-start | bytes 24580
  979.6 113.9 %copy-start.29 = (f32[384]{0:T(512)S(1)}, f32[384]{0:T(512)}, u32[]{:S(2)}) copy-start(f32[384]{0:T(512)} %copy-done.28) | copy-start | bytes 4612
  1049.6 2.8 copy-start.5
  1049.6 2.8 copy-start.12
  (6 other events, 8.0 us)
Sparse Core Ops, SparseCore 0:
  14.1 72.8 all-gather.4
  163.2 70.2 reduce-scatter.10
  235.3 70.1 all-gather.8
  307.7 70.1 all-gather.6
  426.8 70.1 reduce-scatter.14
  499.8 70.1 reduce-scatter.12
  579.0 70.1 all-gather.10
  651.4 89.5 reduce-scatter.26
  743.4 87.9 reduce-scatter.28
  833.5 34.0 reduce-scatter.24
  870.0 34.3 reduce-scatter.18
  906.5 34.5 reduce-scatter.22
  943.4 34.3 reduce-scatter.20
  980.6 68.8 reduce-scatter.16
where the time goes:
time: 1110 us
  waiting for transfers between devices  616 us (55%)
  matrix products  285 us (26%)
  local copies, waits for them, and re-layouts  78.1 us (7%)
  other arithmetic  71.6 us (6%)
  blocking collectives  39.5 us (4%)
  between operations  14.6 us (1%)
    all_gather x1, waiting for transfers between devices, local(): lax.all_gather(normed_attn.astype(jnp.bfloat16), 'mp', axis=0, tiled=True)  73 us
    reduce_scatter x1, waiting for transfers between devices, local(): lax.psum_scatter(attn_input_back(queries_grad, keys_grad, values_grad, qu...  70 us
    reduce_scatter x1, waiting for transfers between devices, local(): lax.psum_scatter(rows_times(context_flat, out_weight).astype(jnp.bfloat16...  69.6 us
    reduce_scatter x1, waiting for transfers between devices, local(): lax.psum_scatter(rows_times(hidden, down_weight).astype(jnp.bfloat16), 'm...  68.7 us
    all_gather x1, waiting for transfers between devices, local(): cotangent_all = lax.all_gather(out_cotangent, 'mp', axis=0, tiled=True)  66.6 us
    all_gather x1, waiting for transfers between devices, local(): lax.all_gather(normed_mlp.astype(jnp.bfloat16), 'mp', axis=0, tiled=True)  53.4 us
    dot_general x4, matrix products, rows_times_back(): lax.dot_general(left_rows, right_matrix, (((1,), (1,)), ((), ())), prefer...  51.6 us
    reduce_scatter x1, waiting for transfers between devices, local(): lax.psum_scatter(rows_times_back(pre_grad, up_weight).astype(jnp.bfloat16...  49.7 us
  transfers between devices with their start and end apart: 14, of which 12 were waited for; matrix products, arithmetic and copies ran while one was open for 25% of the time, Pallas kernels for 0%

commit v1 on v0

--- a/solution.py
+++ b/solution.py
@@ -103,7 +103,17 @@
     flat_shape = (group_rows, head_count * HEAD_DIM)
     residual_in = tokens.astype(jnp.float32)
     normed_attn, attn_norm_back = jax.vjp(norm_rows, residual_in, attn_gain)
-    gathered_attn = lax.all_gather(normed_attn.astype(jnp.bfloat16), "mp", axis=0, tiled=True)
+    x = normed_attn.astype(jnp.bfloat16)
+    ways = lax.axis_size("mp")
+    up = [(d, (d + 1) % ways) for d in range(ways)]
+    down = [(d, (d - 1) % ways) for d in range(ways)]
+    earlier, later = ([x], [x])
+    for _ in range(ways // 2):
+        earlier.append(lax.ppermute(earlier[-1], "mp", up))
+    for _ in range((ways - 1) // 2):
+        later.append(lax.ppermute(later[-1], "mp", down))
+    line = jnp.concatenate([*earlier[::-1], *later[1:]], axis=0)
+    gathered_attn = jnp.roll(line, (lax.axis_index("mp") - ways // 2) * x.shape[0], axis=0)
     queries = (
         jnp.dot(gathered_attn, query_weight, preferred_element_type=jnp.float32) * score_scale
     ).astype(jnp.bfloat16)

time: 1110 us -> 1160 us (1.045)
  waiting for transfers between devices: 616 us -> 642 us
  local copies, waits for them, and re-layouts: 78.1 us -> 90.6 us
    ppermute x0 -> x3, waiting for transfers between devices: none -> 99.6 us  [the longest x2 71.3 us: local(): earlier.append(lax.ppermute(earlier[-1], 'mp', up))]
    all_gather x1 -> x0, waiting for transfers between devices: 73 us -> none  [local(): lax.all_gather(normed_attn.astype(jnp.bfloat16), 'mp', axis=0, tiled=True)]
  transfers between devices with their start and end apart: 14 -> 16, of which waited for: 12 -> 14; matrix products, arithmetic and copies ran while one was open for 25% -> 24% of each run, Pallas kernels for 0% -> 0%
where the time goes in v1:
time: 1160 us; the launch traced here: 1150 us
  waiting for transfers between devices  642 us (55%)
  matrix products  281 us (24%)
  local copies, waits for them, and re-layouts  90.6 us (8%)
  other arithmetic  72.5 us (6%)
  blocking collectives  39.5 us (3%)
  between operations  14.6 us (1%)
    ppermute x2, waiting for transfers between devices, local(): earlier.append(lax.ppermute(earlier[-1], 'mp', up))  71.3 us
    reduce_scatter x1, waiting for transfers between devices, local(): lax.psum_scatter(attn_input_back(queries_grad, keys_grad, values_grad, qu...  70.1 us
    reduce_scatter x1, waiting for transfers between devices, local(): lax.psum_scatter(rows_times(context_flat, out_weight).astype(jnp.bfloat16...  69 us
    reduce_scatter x1, waiting for transfers between devices, local(): lax.psum_scatter(rows_times(hidden, down_weight).astype(jnp.bfloat16), 'm...  68.7 us
    all_gather x1, waiting for transfers between devices, local(): cotangent_all = lax.all_gather(out_cotangent, 'mp', axis=0, tiled=True)  66.6 us
    all_gather x1, waiting for transfers between devices, local(): lax.all_gather(normed_mlp.astype(jnp.bfloat16), 'mp', axis=0, tiled=True)  53.2 us
    dot_general x4, matrix products, rows_times_back(): lax.dot_general(left_rows, right_matrix, (((1,), (1,)), ((), ())), prefer...  51.5 us
    reduce_scatter x1, waiting for transfers between devices, local(): lax.psum_scatter(rows_times_back(pre_grad, up_weight).astype(jnp.bfloat16...  49.8 us
  transfers between devices with their start and end apart: 16, of which 14 were waited for; matrix products, arithmetic and copies ran while one was open for 24% of the time, Pallas kernels for 0%

profile of v1, /device:TPU:0, one launch (start us, length us, event | category | flops | bytes accessed | tf_op | source)
XLA Modules:
  0.0 1148.4 jit_solution(927101373010233394)
XLA Ops:
  16.3 35.7 %collective-permute-done = bf16[384,2048]{1,0:T(8,128)(2,1)} collective-permute-done((bf16[384,2048]{1,0:T(8,128)(2,1)}, bf16[384,2048]{1,0:T(8,128)(2,1)}, u32[]{:S(2)}, u32[]{:S(2)}) %collective-permute-start) | collective-permute-done | bytes 1572896 | tf_op jit(solution)/shard_map/ppermute | solution.py:112
  54.9 35.6 %collective-permute-done.1 = bf16[384,2048]{1,0:T(8,128)(2,1)} collective-permute-done((bf16[384,2048]{1,0:T(8,128)(2,1)}, bf16[384,2048]{1,0:T(8,128)(2,1)}, u32[]{:S(2)}, u32[]{:S(2)}) %collective-permute-start.1) | collective-permute-done | bytes 1572896 | tf_op jit(solution)/shard_map/ppermute | solution.py:112
  94.1 28.3 %collective-permute-done.2 = bf16[384,2048]{1,0:T(8,128)(2,1)} collective-permute-done((bf16[384,2048]{1,0:T(8,128)(2,1)}, bf16[384,2048]{1,0:T(8,128)(2,1)}, u32[]{:S(2)}, u32[]{:S(2)}) %collective-permute-start.2) | collective-permute-done | bytes 1572896 | tf_op jit(solution)/shard_map/ppermute | solution.py:114
  129.1 4.5 copy-done.19
  133.6 4.5 fusion.63
  144.5 7.5 convolution_convert_fusion.11
  158.5 7.5 convolution_convert_fusion.12
  171.0 28.4 %while.26 = (s32[]{:T(128)}, bf16[2,768,4,128]{3,2,1,0:T(4,128)(2,1)}, f32[2,4,768]{2,1,0:T(4,128)S(1)}, bf16[2,768,4,128]{3,2,1,0:T(4,128)(2,1)}, s32[2,768]{1,...) while((s32[]{:T(128)}, ...), condition=%wide.region_5.6_spmd, body=%wide.region_2.5_spmd.sunk | while | flops 1231352832 | bytes 43362440 | solution.py:129
  179.0 3.6 fusion.143
  193.1 3.6 fusion.143
  199.4 6.7 convolution_convert_fusion.6
  207.0 69.0 %reduce-scatter.11.cloned.1.call-done = bf16[384,2048]{1,0:T(8,128)(2,1)} async-done(((bf16[1536,2048]{1,0:T(8,128)(2,1)}), bf16[384,2048]{1,0:T(8,128)(2,1)}) %reduce-scatter.11.cloned.1.call-update) | async-done | bytes 1572880 | tf_op jit(solution)/shard_map/reduce_scatter | solution.py:131
  281.4 66.6 %all-gather.6.cloned.1.call-done = bf16[1536,2048]{1,0:T(8,128)(2,1)} async-done(((bf16[384,2048]{1,0:T(8,128)(2,1)}), bf16[1536,2048]{1,0:T(8,128)(2,1)}) %all-gather.6.cloned.1.call-update) | async-done | bytes 6291472 | tf_op jit(solution)/shard_map/all_gather | solution.py:147
  348.0 19.5 %fusion.101 = f32[1536,2048]{1,0:T(8,128)} fusion(bf16[1536,2048]{1,0:T(8,128)(2,1)} %all-gather.6.cloned.1.call-done, bf16[2048,2048]{1,0:T(8,128)(2,1)} %param.22), kind=kOutput, calls=%fused_computation.166 | convolution fusion | flops 12884901888 | bytes 27262976 | tf_op jit(solution)/shard_map/dot_general | solution.py:151
  367.4 53.2 %all-gather.4.cloned.1.call-done = bf16[1536,2048]{1,0:T(8,128)(2,1)} async-done(((bf16[384,2048]{1,0:T(8,128)(2,1)}), bf16[1536,2048]{1,0:T(8,128)(2,1)}) %all-gather.4.cloned.1.call-update) | async-done | bytes 6291472 | tf_op jit(solution)/shard_map/all_gather | solution.py:139
  420.6 29.6 %fusion.48 = (bf16[1536,2048]{1,0:T(8,128)(2,1)}, f32[1536,2048]{1,0:T(8,128)}) fusion(f32[1536,2048]{1,0:T(8,128)} %fusion.101, bf16[1536,2048]{1,0:T(8,128)(2,1)} %all-gather.4.cloned.1.call-done, bf16[2048,2048]{1,0:T(8,128)(2,1)} %param.21), kind=kOutput, calls=%fused_computation.68 | convolution fusion | flops 12947816448 | bytes 46137344 | tf_op jit(solution)/shard_map/dot_general | solution.py:140
  450.2 19.2 %convolution_convert_fusion.4 = bf16[1536,2048]{1,0:T(8,128)(2,1)} fusion(bf16[1536,2048]{1,0:T(8,128)(2,1)} %get-tuple-element.190, bf16[2048,2048]{1,0:T(8,128)(2,1)} %param.21), kind=kOutput, calls=%fused_computation.73 | convolution fusion | flops 12888047616 | bytes 20971520 | tf_op jit(solution)/shard_map/dot_general | solution.py:33
  469.4 20.5 %convolution_convert_fusion.5 = bf16[1536,2048]{1,0:T(8,128)(2,1)} fusion(bf16[2048,2048]{1,0:T(8,128)(2,1)} %param.22, f32[1536,2048]{1,0:T(8,128)} %get-tuple-element.191), kind=kOutput, calls=%fused_computation.74 | convolution fusion | flops 12916359168 | bytes 27262976 | tf_op jit(solution)/shard_map/dot_general | solution.py:29
  490.0 49.8 %reduce-scatter.15.cloned.1.call-done = bf16[384,2048]{1,0:T(8,128)(2,1)} async-done(((bf16[1536,2048]{1,0:T(8,128)(2,1)}), bf16[384,2048]{1,0:T(8,128)(2,1)}) %reduce-scatter.15.cloned.1.call-update) | async-done | bytes 1572880 | tf_op jit(solution)/shard_map/reduce_scatter | solution.py:158
  539.7 4.4 fusion.59
  544.1 68.7 %reduce-scatter.13.cloned.1.call-done = bf16[384,2048]{1,0:T(8,128)(2,1)} async-done(((bf16[1536,2048]{1,0:T(8,128)(2,1)}), bf16[384,2048]{1,0:T(8,128)(2,1)}) %reduce-scatter.13.cloned.1.call-update) | async-done | bytes 1572880 | tf_op jit(solution)/shard_map/reduce_scatter | solution.py:143
  612.8 5.5 fusion.100
  621.6 19.6 %convolution_convert_fusion.3 = bf16[2048,2048]{1,0:T(8,128)(2,1)} fusion(bf16[1536,2048]{1,0:T(8,128)(2,1)} %all-gather.4.cloned.1.call-done, bf16[1536,2048]{1,0:T(8,128)(2,1)} %get-tuple-element.190), kind=kOutput, calls=%fused_computation.72 | convolution fusion | flops 12889096192 | bytes 20971520 | tf_op jit(solution)/shard_map/rd,rf->df/dot_general | solution.py:155
  641.3 22.6 %convolution_convert_fusion.2 = bf16[2048,2048]{1,0:T(8,128)(2,1)} fusion(bf16[1536,2048]{1,0:T(8,128)(2,1)} %all-gather.6.cloned.1.call-done, f32[1536,2048]{1,0:T(8,128)} %get-tuple-element.191), kind=kOutput, calls=%fused_computation.71 | convolution fusion | flops 12917407744 | bytes 27262976 | tf_op jit(solution)/shard_map/rf,rd->fd/dot_general | solution.py:148
  664.0 27.9 %all-gather.8.cloned.1.call-done = bf16[1536,2048]{1,0:T(8,128)(2,1)} async-done(((bf16[384,2048]{1,0:T(8,128)(2,1)}), bf16[1536,2048]{1,0:T(8,128)(2,1)}) %all-gather.8.cloned.1.call-update) | async-done | bytes 6291472 | tf_op jit(solution)/shard_map/all_gather | solution.py:166
  691.9 7.9 convolution_convert_fusion.10
  699.7 3.6 reshape.218
  703.4 8.1 convolution_convert_fusion.7
  716.3 99.1 %while.27 = (s32[]{:T(128)}, bf16[2,768,4,128]{3,2,1,0:T(4,128)(2,1)}, bf16[2,768,4,128]{3,2,1,0:T(4,128)(2,1)}, bf16[2,768,4,128]{3,2,1,0:T(4,128)(2,1)}, bf16[...) while((s32[]{:T(128)}, ...), condition=%wide.region_15.16_spmd, body=%wide.region_13.15_spmd.sunk | while | flops 3051156480 | bytes 169179440 | solution.py:173
  731.5 8.0 multiply_reduce_fusion.3
  739.5 10.8 multiply_convert_fusion.7
  750.3 4.4 fusion.155
  780.6 8.0 multiply_reduce_fusion.3
  788.5 11.4 multiply_convert_fusion.7
  800.0 4.5 fusion.155
  815.4 8.1 multiply_convert_fusion.2
  823.6 8.2 convolution_convert_fusion.8
  831.8 8.1 convolution_convert_fusion.9
  840.3 10.2 fusion.78
  850.5 6.3 fusion.75
  856.9 15.8 %add_convert_fusion = bf16[1536,2048]{1,0:T(8,128)(2,1)} fusion(f32[1536,2048]{1,0:T(8,128)} %fusion.75, f32[1536,2048]{1,0:T(8,128)} %fusion.78, bf16[2048,512]{1,0:T(8,128)(2,1)} %param.17, bf16[192,8,4,128]{3,2,1,0:T(4,128)(2,1)} %bitcast.141), kind=kOutput, calls=%fused_computation.69 | convolution fusion | flops 3233808384 | bytes 35127296 | tf_op jit(solution)/shard_map/dot_general | solution.py:33
  878.2 32.4 %reduce-scatter.25.cloned.1.call-done = bf16[512,256]{1,0:T(8,128)(2,1)} async-done(((bf16[512,2048]{1,0:T(8,128)(2,1)}), bf16[512,256]{1,0:T(8,128)(2,1)}) %reduce-scatter.25.cloned.1.call-update) | async-done | bytes 262160 | tf_op jit(solution)/shard_map/reduce_scatter | solution.py:224
  912.4 34.7 %reduce-scatter.19.cloned.1.call-done = bf16[256,512]{1,0:T(8,128)(2,1)} async-done(((bf16[2048,512]{1,0:T(8,128)(2,1)}), bf16[256,512]{1,0:T(8,128)(2,1)}) %reduce-scatter.19.cloned.1.call-update) | async-done | bytes 262160 | tf_op jit(solution)/shard_map/reduce_scatter | solution.py:215
  948.9 34.9 %reduce-scatter.23.cloned.1.call-done = bf16[256,512]{1,0:T(8,128)(2,1)} async-done(((bf16[2048,512]{1,0:T(8,128)(2,1)}), bf16[256,512]{1,0:T(8,128)(2,1)}) %reduce-scatter.23.cloned.1.call-update) | async-done | bytes 262160 | tf_op jit(solution)/shard_map/reduce_scatter | solution.py:221
  985.6 34.9 %reduce-scatter.21.cloned.1.call-done = bf16[256,512]{1,0:T(8,128)(2,1)} async-done(((bf16[2048,512]{1,0:T(8,128)(2,1)}), bf16[256,512]{1,0:T(8,128)(2,1)}) %reduce-scatter.21.cloned.1.call-update) | async-done | bytes 262160 | tf_op jit(solution)/shard_map/reduce_scatter | solution.py:218
  1022.3 70.1 %reduce-scatter.17.cloned.1.call-done = bf16[384,2048]{1,0:T(8,128)(2,1)} async-done(((bf16[1536,2048]{1,0:T(8,128)(2,1)}), bf16[384,2048]{1,0:T(8,128)(2,1)}) %reduce-scatter.17.cloned.1.call-update) | async-done | bytes 1572880 | tf_op jit(solution)/shard_map/reduce_scatter | solution.py:190
  1096.8 39.5 %all-reduce = (f32[2048]{0:T(1024)}, f32[2048]{0:T(1024)}) all-reduce(f32[2048]{0:T(1024)S(1)} %get-tuple-element.143, f32[2048]{0:T(1024)S(1)} %copy-done.29), channel_id=1, replica_groups=mesh['dp'=8,'mp'=4] {'dp','mp'}, use_global_device_ids=true, to_apply=%region_26.27 | all-reduce | flops 4096 | bytes 32768 | tf_op jit(solution)/shard_map/psum | solution.py:206
  1136.3 5.1 add_add_fusion.2
  (201 shorter events, 144.5 us)
Async XLA Ops:
  7.2 192.2 %copy-start = (bf16[512,2048]{1,0:T(8,128)(2,1)S(1)}, bf16[512,2048]{1,0:T(8,128)(2,1)}, u32[]{:S(2)}) copy-start(bf16[512,2048]{1,0:T(8,128)(2,1)} %param.20) | copy-start | bytes 6291460
  7.2 4.5 copy-start.17
  7.2 268.8 %reduce-scatter.11.cloned.1.call-start = ((), (), s32[]{:S(2)}) async-start(), calls=%async_computation.10 | async-start | bytes 7864320 | tf_op jit(solution)/shard_map/reduce_scatter | solution.py:131
  7.2 4.4 copy-start.3
  9.1 117.8 %copy-start.24 = (f32[384]{0:T(512)}, f32[384]{0:T(512)S(1)}, u32[]{:S(2)}) copy-start(f32[384]{0:T(512)S(1)} %broadcast_multiply_fusion.1) | copy-start | bytes 4612
  11.7 115.3 %copy-start.26 = (f32[384]{0:T(512)}, f32[384]{0:T(512)S(1)}, u32[]{:S(2)}) copy-start(f32[384]{0:T(512)S(1)} %fusion.92) | copy-start | bytes 4612
  13.4 38.6 %collective-permute-start = (bf16[384,2048]{1,0:T(8,128)(2,1)}, bf16[384,2048]{1,0:T(8,128)(2,1)}, u32[]{:S(2)}, u32[]{:S(2)}) collective-permute-start(bf16[384,2048]{1,0:T(8,128)(2,1)} %fusion.57), channel_id=1, source_target_pairs={{0,1},{1,2},{2,3},{3,0},{4,5},{5,6},{6,7},{7,4},{8,9},{9,10},{10,1... | collective-permute-start | bytes 4718600 | tf_op jit(solution)/shard_map/ppermute | solution.py:112
  52.0 38.5 %collective-permute-start.1 = (bf16[384,2048]{1,0:T(8,128)(2,1)}, bf16[384,2048]{1,0:T(8,128)(2,1)}, u32[]{:S(2)}, u32[]{:S(2)}) collective-permute-start(bf16[384,2048]{1,0:T(8,128)(2,1)} %collective-permute-done), channel_id=1, source_target_pairs={{0,1},{1,2},{2,3},{3,0},{4,5},{5,6},{6,7},{7,4},{8,9},{9,10},{10,1... | collective-permute-start | bytes 4718600 | tf_op jit(solution)/shard_map/ppermute | solution.py:112
  52.8 69.6 %collective-permute-start.2 = (bf16[384,2048]{1,0:T(8,128)(2,1)}, bf16[384,2048]{1,0:T(8,128)(2,1)}, u32[]{:S(2)}, u32[]{:S(2)}) collective-permute-start(bf16[384,2048]{1,0:T(8,128)(2,1)} %fusion.57), channel_id=1, source_target_pairs={{0,3},{1,0},{2,1},{3,2},{4,7},{5,4},{6,5},{7,6},{8,11},{9,8},{10,9... | collective-permute-start | bytes 4718600 | tf_op jit(solution)/shard_map/ppermute | solution.py:114
  54.9 38.7 %copy-start.4 = (bf16[384,2048]{1,0:T(8,128)(2,1)S(1)}, bf16[384,2048]{1,0:T(8,128)(2,1)}, u32[]{:S(2)}) copy-start(bf16[384,2048]{1,0:T(8,128)(2,1)} %param.15) | copy-start | bytes 4718596
  127.0 6.7 copy-start.15
  129.1 4.5 copy-start.19
  166.0 5.1 copy-start.22
  199.4 6.8 copy-start.20
  206.2 141.8 %all-gather.6.cloned.1.call-start = ((), (), s32[]{:S(2)}) async-start(), calls=%async_computation.13 | async-start | bytes 7864320 | tf_op jit(solution)/shard_map/all_gather | solution.py:147
  206.2 73.3 %copy-start.28 = (f32[2048]{0:T(1024)S(1)}, f32[2048]{0:T(1024)}, u32[]{:S(2)}) copy-start(f32[2048]{0:T(1024)} %param.24) | copy-start | bytes 24580
  206.9 213.7 %all-gather.4.cloned.1.call-start = ((), (), s32[]{:S(2)}) async-start(), calls=%async_computation.11 | async-start | bytes 7864320 | tf_op jit(solution)/shard_map/all_gather | solution.py:139
  281.4 258.4 %reduce-scatter.15.cloned.1.call-start = ((), (), s32[]{:S(2)}) async-start(), calls=%async_computation.14 | async-start | bytes 7864320 | tf_op jit(solution)/shard_map/reduce_scatter | solution.py:158
  469.4 143.4 %reduce-scatter.13.cloned.1.call-start = ((), (), s32[]{:S(2)}) async-start(), calls=%async_computation.12 | async-start | bytes 7864320 | tf_op jit(solution)/shard_map/reduce_scatter | solution.py:143
  489.9 202.0 %all-gather.8.cloned.1.call-start = ((), (), s32[]{:S(2)}) async-start(), calls=%async_computation.15 | async-start | bytes 7864320 | tf_op jit(solution)/shard_map/all_gather | solution.py:166
  612.8 7.2 copy-start.14
  621.6 251.1 %reduce-scatter.27.cloned.1.call-start = ((), (), s32[]{:S(2)}) async-start(), calls=%async_computation.21 | async-start | bytes 9437184 | tf_op jit(solution)/shard_map/reduce_scatter | solution.py:227
  641.2 234.2 %reduce-scatter.29.cloned.1.call-start = ((), (), s32[]{:S(2)}) async-start(), calls=%async_computation.22 | async-start | bytes 9437184 | tf_op jit(solution)/shard_map/reduce_scatter | solution.py:230
  663.9 246.7 %reduce-scatter.25.cloned.1.call-start = ((), (), s32[]{:S(2)}) async-start(), calls=%async_computation.20 | async-start | bytes 2359296 | tf_op jit(solution)/shard_map/reduce_scatter | solution.py:224
  711.5 4.8 copy-start.21
  711.5 4.8 copy-start.23
  711.5 235.5 %reduce-scatter.19.cloned.1.call-start = ((), (), s32[]{:S(2)}) async-start(), calls=%async_computation.17 | async-start | bytes 2359296 | tf_op jit(solution)/shard_map/reduce_scatter | solution.py:215
  716.4 4.4 copy-start.7
  716.4 4.4 copy-start.8
  722.2 3.5 copy-start.1
  750.3 4.4 copy-start.2
  750.3 4.6 copy-start.9
  765.5 4.4 copy-start.7
  765.5 4.4 copy-start.8
  771.3 3.5 copy-start.1
  800.0 4.5 copy-start.2
  800.0 4.6 copy-start.9
  823.5 160.2 %reduce-scatter.23.cloned.1.call-start = ((), (), s32[]{:S(2)}) async-start(), calls=%async_computation.19 | async-start | bytes 2359296 | tf_op jit(solution)/shard_map/reduce_scatter | solution.py:221
  831.8 188.7 %reduce-scatter.21.cloned.1.call-start = ((), (), s32[]{:S(2)}) async-start(), calls=%async_computation.18 | async-start | bytes 2359296 | tf_op jit(solution)/shard_map/reduce_scatter | solution.py:218
  840.0 252.3 %reduce-scatter.17.cloned.1.call-start = ((), (), s32[]{:S(2)}) async-start(), calls=%async_computation.16 | async-start | bytes 7864320 | tf_op jit(solution)/shard_map/reduce_scatter | solution.py:190
  840.3 10.2 copy-start.16
  840.3 10.2 copy-start.36
  875.5 216.8 %copy-start.18 = (f32[2048]{0:T(1024)S(1)}, f32[2048]{0:T(1024)}, u32[]{:S(2)}) copy-start(f32[2048]{0:T(1024)} %param.23) | copy-start | bytes 24580
  875.5 216.8 %copy-start.25 = (f32[384]{0:T(512)S(1)}, f32[384]{0:T(512)}, u32[]{:S(2)}) copy-start(f32[384]{0:T(512)} %copy-done.24) | copy-start | bytes 4612
  878.2 216.9 %copy-start.33 = (f32[384]{0:T(512)S(1)}, f32[384]{0:T(512)}, u32[]{:S(2)}) copy-start(f32[384]{0:T(512)} %copy-done.32) | copy-start | bytes 4612
  878.2 216.9 %copy-start.27 = (f32[384]{0:T(512)S(1)}, f32[384]{0:T(512)}, u32[]{:S(2)}) copy-start(f32[384]{0:T(512)} %copy-done.26) | copy-start | bytes 4612
  1022.3 74.5 %copy-start.29 = (f32[2048]{0:T(1024)S(1)}, f32[2048]{0:T(1024)}, u32[]{:S(2)}) copy-start(f32[2048]{0:T(1024)} %get-tuple-element.141) | copy-start | bytes 24580
  1022.3 114.0 %copy-start.31 = (f32[384]{0:T(512)S(1)}, f32[384]{0:T(512)}, u32[]{:S(2)}) copy-start(f32[384]{0:T(512)} %copy-done.30) | copy-start | bytes 4612
  (11 other events, 24.3 us)
Sparse Core Ops, SparseCore 0:
  206.3 69.6 reduce-scatter.10
  277.8 70.1 all-gather.5
  350.4 70.1 all-gather.3
  469.5 70.2 reduce-scatter.14
  542.6 70.1 reduce-scatter.12
  621.7 70.1 all-gather.7
  694.2 89.5 reduce-scatter.26
  786.1 87.9 reduce-scatter.28
  876.4 34.1 reduce-scatter.24
  912.8 34.2 reduce-scatter.18
  949.4 34.3 reduce-scatter.22
  985.9 34.4 reduce-scatter.20
  1023.4 68.8 reduce-scatter.16
